TPU v7x, 128 devices: a whole 4x4x4 slice. The times are simulated.
128 devices in a mesh: row: 8 (over y, core), col: 16 (over z, x).
Axes of the slice: x: 4, y: 4, z: 4, core: 2. Of those that a mesh axis runs over, the one named last changes fastest.
Arguments:
- ancestor_inverse: float32 [12288, 12288], P('row', 'col')
- factor: bfloat16 [3, 12288, 512], P(None, ('row', 'col')), may hold values from -0.5 to 0.5
- coupling: float32 [3, 512, 512], replicated, may hold values from -0.25 to 0.25
- diagonal_inverse: float32 [3, 512, 512], replicated, may hold values from -6 to 6
- ancestors: int32 [3, 24], replicated, may hold values from -1 to 23, as said below
Outputs:
- block_columns: float32 [3, 12288, 512], P(None, ('row', 'col'))
- block_rows: float32 [3, 12288, 512], P(None, ('col', 'row'))
- node_blocks: float32 [3, 3, 512, 512], replicated
Inputs may be any that keep to these rules, and one draw needn't show every extreme that they name: `ancestors`: row k lists the ancestor block rows of supernode k, blocks of 512 rows: distinct indices in increasing order, then -1 in the slots left. Every block is listed by some supernode.
All inputs are finite; a program needn't handle non-finite values.
Results may differ from a plain program's by a relative error of at most 0.0003.
Values may be sent and summed in bfloat16 or wider, within the bound.
A program may use at most 128 MiB of HBM per device.

v0:
```python
import jax
import jax.numpy as jnp
from jax import lax
from jax.sharding import PartitionSpec as P

highest = lax.Precision.HIGHEST


def broadcast(value, axis, source):
    kept = jnp.where(lax.axis_index(axis) == source, value, 0).astype(value.dtype)
    return lax.psum(kept, axis)


def matmul(left, right):
    return jnp.dot(left, right, precision=highest)


def left_dot(left, right):
    return lax.dot_general(left, right, (((0,), (0,)), ((), ())), precision=highest)


def pair_index(later, earlier):
    return later * (later - 1) // 2 + earlier


def local(ancestor_inverse, factor, coupling, diagonal_inverse, ancestors):
    col_count = lax.axis_size("col")
    row_count = lax.axis_size("row")
    row_index = lax.axis_index("row")
    col_index = lax.axis_index("col")
    nodes_total, piece_rows, sn_width = factor.shape
    rows_here, cols_here = ancestor_inverse.shape
    group_ratio = rows_here // cols_here
    first_row = (row_index * col_count + col_index) * piece_rows
    block_of_row = (first_row + jnp.arange(piece_rows, dtype=jnp.int32)) // sn_width
    source_row = col_index // group_ratio
    block_start = col_index % group_ratio * cols_here
    row_layout = []
    solved = {}
    for current in range(nodes_total):
        listed = jnp.any(ancestors[current][:, None] == block_of_row[None, :], axis=0)
        lower_part = jnp.where(listed[:, None], factor[current], jnp.zeros_like(factor[current]))
        lower_rows = lax.all_gather(lower_part, "col", axis=0, tiled=True)
        own_block = lax.dynamic_slice_in_dim(lower_rows, block_start, cols_here, 0)
        lower_cols = broadcast(own_block, "row", source_row).astype(jnp.float32)
        lower_here = lower_part.astype(jnp.float32)
        product_sum = lax.psum_scatter(
            matmul(ancestor_inverse, lower_cols), "col", scatter_dimension=0, tiled=True
        )
        for earlier in range(current):
            product_sum = product_sum + matmul(
                row_layout[earlier], coupling[pair_index(current, earlier)]
            )
        column = -product_sum
        stacked = jnp.concatenate(row_layout + [column], axis=1)
        summed = lax.psum(left_dot(lower_here, stacked), ("row", "col"))
        crosses = [
            summed[:, earlier * sn_width : (earlier + 1) * sn_width] for earlier in range(current)
        ]
        self_term = summed[:, current * sn_width : (current + 1) * sn_width]
        for earlier in range(current):
            block_value = -crosses[earlier].T
            for inner in range(current):
                block_value = block_value - matmul(
                    solved[earlier, inner], coupling[pair_index(current, inner)]
                )
            solved[earlier, current] = block_value
            solved[current, earlier] = block_value.T
        diag_value = diagonal_inverse[current] - self_term
        for earlier in range(current):
            diag_value = diag_value - left_dot(
                coupling[pair_index(current, earlier)], solved[earlier, current]
            )
        solved[current, current] = diag_value
        row_layout.append(column)
    finished = jnp.stack(row_layout)
    part_rows = piece_rows // row_count
    ratio_cols = col_count // row_count
    split_parts = finished.reshape(nodes_total, row_count, part_rows, sn_width)
    held = lax.all_to_all(split_parts, "row", split_axis=1, concat_axis=1, tiled=True)
    targets = jnp.arange(row_count, dtype=jnp.int32) * ratio_cols + col_index // row_count
    onehot = (targets[:, None] == jnp.arange(col_count, dtype=jnp.int32)[None, :]).astype(
        jnp.float32
    )
    slotted = jnp.einsum("rc,nrqs->ncqs", onehot, held, precision=highest)
    arrived = lax.all_to_all(slotted, "col", split_axis=1, concat_axis=1, tiled=True)
    picked = lax.dynamic_slice_in_dim(arrived, col_index % ratio_cols * row_count, row_count, 1)
    landed = lax.all_to_all(picked, "row", split_axis=1, concat_axis=1, tiled=True)
    mirrored_all = landed.reshape(nodes_total, piece_rows, sn_width)
    node_blocks = jnp.stack(
        [
            jnp.stack([solved[first_node, second_node] for second_node in range(nodes_total)])
            for first_node in range(nodes_total)
        ]
    )
    return (finished, mirrored_all, node_blocks)


def solution(mesh):
    placed = (P("row", "col"), P(None, ("row", "col"), None), P(), P(), P())
    return jax.shard_map(
        local,
        mesh=mesh,
        in_specs=placed,
        out_specs=(P(None, ("row", "col"), None), P(None, ("col", "row"), None), P()),
        check_vma=False,
    )
```

profile of v0, /device:TPU:1, one launch (start us, length us, event | category | flops | bytes accessed | tf_op | source)
XLA Modules:
  0.0 691.0 jit_solution(10552824575240240170)
XLA Ops:
  7.2 0.8 slice_bitcast_fusion.2
  8.1 1.8 bitcast_select_fusion.1
  10.0 0.7 all-gather.4.cloned.1.call-update
  11.5 45.6 %all-gather.6.cloned.1.call-done = bf16[1536,512]{1,0:T(8,128)(2,1)} async-done(((bf16[96,512]{1,0:T(8,128)(2,1)}), bf16[1536,512]{1,0:T(8,128)(2,1)}) %all-gather.6.cloned.1.call-update) | async-done | bytes 1572880 | tf_op jit(solution)/shard_map/all_gather | solution.py:43
  57.1 2.2 dynamic-slice_select_fusion.1
  59.2 43.3 %all-gather.4.cloned.1.call-done = bf16[1536,512]{1,0:T(8,128)(2,1)} async-done(((bf16[96,512]{1,0:T(8,128)(2,1)}), bf16[1536,512]{1,0:T(8,128)(2,1)}) %all-gather.4.cloned.1.call-update) | async-done | bytes 1572880 | tf_op jit(solution)/shard_map/all_gather | solution.py:43
  102.5 2.1 dynamic-slice_select_fusion.2
  104.7 43.3 %all-gather.8.cloned.1.call-done = bf16[1536,512]{1,0:T(8,128)(2,1)} async-done(((bf16[96,512]{1,0:T(8,128)(2,1)}), bf16[1536,512]{1,0:T(8,128)(2,1)}) %all-gather.8.cloned.1.call-update) | async-done | bytes 1572880 | tf_op jit(solution)/shard_map/all_gather | solution.py:43
  148.0 2.1 dynamic-slice_select_fusion
  150.3 66.0 %all-reduce.7.cloned.1.call-done = (bf16[768,512]{1,0:T(8,128)(2,1)}, bf16[768,512]{1,0:T(8,128)(2,1)}, bf16[768,512]{1,0:T(8,128)(2,1)}) async-done(((bf16[768,512]{1,0:T(8,128)(2,1)}, bf16[768,512]{1,0:T(8,128)(2,1)}, bf16[768,512]{1,0:T(8,128)(2,1)}), (bf16[768,512]{1,0:T(8,128)(2,1)}, bf16[768,512]{1,0:T(8,128)(2,1)}, bf16[768,512]{1,0:T(8,128)(2,1)})) %all-reduce.7.cloned.1.call-update) | async-done | bytes 2359312 | tf_op jit(solution)/shard_map/psum | solution.py:11
  216.2 6.7 convolution_bitcast_fusion.2
  222.9 2.3 copy.104
  225.3 6.7 convolution_bitcast_fusion.1
  232.0 2.4 copy.106
  234.5 6.7 convolution_bitcast_fusion
  241.2 2.4 copy.108
  244.1 57.1 %reduce-scatter.10.cloned.1.call-done = f32[96,512]{1,0:T(8,128)} async-done(((f32[1536,512]{1,0:T(8,128)}), f32[96,512]{1,0:T(8,128)}) %reduce-scatter.10.cloned.1.call-update) | async-done | bytes 196624 | tf_op jit(solution)/shard_map/reduce_scatter | solution.py:47
  301.2 78.3 %reduce-scatter.12.cloned.1.call-done = f32[96,512]{1,0:T(8,128)} async-done(((f32[1536,512]{1,0:T(8,128)}), f32[96,512]{1,0:T(8,128)}) %reduce-scatter.12.cloned.1.call-update) | async-done | bytes 196624 | tf_op jit(solution)/shard_map/reduce_scatter | solution.py:47
  379.5 1.8 fusion.5
  381.3 77.3 %reduce-scatter.14.cloned.1.call-done = f32[96,512]{1,0:T(8,128)} async-done(((f32[1536,512]{1,0:T(8,128)}), f32[96,512]{1,0:T(8,128)}) %reduce-scatter.14.cloned.1.call-update) | async-done | bytes 196624 | tf_op jit(solution)/shard_map/reduce_scatter | solution.py:47
  458.6 1.8 convolution_add_fusion.1
  460.4 0.7 fusion.4
  461.2 0.7 fusion.63
  461.9 2.3 fusion.45
  464.2 3.1 fusion.38
  467.4 1.6 fusion.54
  469.0 0.9 copy-done.18
  469.9 0.7 stack.74
  470.6 0.7 stack.73
  471.4 1.6 stack.72
  473.0 1.2 pad_maximum_fusion.1
  474.2 1.0 copy.78
  475.2 6.7 all-to-all-start
  481.9 15.6 %all-to-all-done = f32[3,8,12,512]{3,2,0,1:T(8,128)} async-done(((f32[3,8,12,512]{3,2,0,1:T(8,128)}), f32[3,8,12,512]{3,2,0,1:T(8,128)}, u32[]{:S(2)}, u32[]{:S(2)}) %all-to-all-start) | async-done | bytes 589856 | tf_op jit(solution)/shard_map/all_to_all | solution.py:80
  497.5 2.1 convolution_bitcast_fusion.3
  499.6 1.9 copy.80
  501.5 4.8 all-to-all-start.1
  506.3 21.0 %all-to-all-done.1 = f32[3,16,12,512]{3,2,0,1:T(8,128)} async-done(((f32[3,16,12,512]{3,2,0,1:T(8,128)}), f32[3,16,12,512]{3,2,0,1:T(8,128)}, u32[]{:S(2)}, u32[]{:S(2)}) %all-to-all-start.1) | async-done | bytes 1179680 | tf_op jit(solution)/shard_map/all_to_all | solution.py:86
  527.3 2.1 constant_dynamic-slice_fusion
  529.4 9.0 %all-to-all-start.2 = ((f32[3,8,12,512]{3,2,0,1:T(8,128)}), f32[3,8,12,512]{3,2,0,1:T(8,128)}, u32[]{:S(2)}, u32[]{:S(2)}) async-start(f32[3,8,12,512]{3,2,0,1:T(8,128)} %constant_dynamic-slice_fusion), calls=%async_computation.2 | async-start | bytes 1572864 | tf_op jit(solution)/shard_map/all_to_all | solution.py:88
  538.4 2.4 slice.71
  540.8 2.6 copy.110
  543.4 1.8 pad_maximum_fusion.2
  545.1 5.7 all-to-all-done.2
  550.9 2.2 copy.81
  553.0 2.0 reshape.46
  555.1 83.9 %all-reduce.5.cloned.1.call-done = (f32[512,1536]{1,0:T(8,128)}, f32[512,512]{1,0:T(8,128)}, f32[512,1024]{0,1:T(8,128)}) async-done(((f32[512,1536]{1,0:T(8,128)}, f32[512,512]{1,0:T(8,128)}, f32[512,1024]{0,1:T(8,128)}), (f32[512,1536]{1,0:T(8,128)}, f32[512,512]{1,0:T(8,128)}, f32[512,1024]{0,1:T(8,128)})) %all-reduce.5.cloned.1.call-update) | async-done | bytes 6291472 | tf_op jit(solution)/shard_map/psum | solution.py:56
  638.9 3.8 bitcast_subtract_fusion.7
  642.7 1.9 fusion.14
  644.6 1.9 fusion.18
  646.6 1.9 fusion.20
  648.5 2.0 fusion.3
  650.5 1.0 copy-done.7
  651.5 2.1 fusion.12
  653.7 3.1 fusion.2
  656.8 2.3 fusion.7
  659.1 2.3 fusion.60
  661.4 2.6 copy.85
  663.9 3.8 maximum_bitcast_fusion.1
  667.8 3.6 copy.95
  671.3 4.3 fusion.1
  676.0 0.9 copy-done.13
  677.5 1.6 copy-done.5
  679.1 4.9 pad_maximum_fusion
  (62 shorter events, 2.7 us)
Async XLA Ops:
  7.2 49.9 %all-gather.6.cloned.1.call-start = ((), (), s32[]{:S(2)}) async-start(), calls=%async_computation.7 | async-start | bytes 1671168 | tf_op jit(solution)/shard_map/all_gather | solution.py:43
  9.9 92.6 %all-gather.4.cloned.1.call-start = ((), (), s32[]{:S(2)}) async-start(), calls=%async_computation.6 | async-start | bytes 1671168 | tf_op jit(solution)/shard_map/all_gather | solution.py:43
  10.7 137.4 %all-gather.8.cloned.1.call-start = ((), (), s32[]{:S(2)}) async-start(), calls=%async_computation.8 | async-start | bytes 1671168 | tf_op jit(solution)/shard_map/all_gather | solution.py:43
  11.4 204.8 %all-reduce.7.cloned.1.call-start = ((), (), s32[]{:S(2)}) async-start(), calls=%async_computation.13 | async-start | bytes 4718592 | tf_op jit(solution)/shard_map/psum | solution.py:11
  150.2 151.0 %reduce-scatter.10.cloned.1.call-start = ((), (), s32[]{:S(2)}) async-start(), calls=%async_computation.9 | async-start | bytes 3342336 | tf_op jit(solution)/shard_map/reduce_scatter | solution.py:47
  225.3 154.3 %reduce-scatter.12.cloned.1.call-start = ((), (), s32[]{:S(2)}) async-start(), calls=%async_computation.10 | async-start | bytes 3342336 | tf_op jit(solution)/shard_map/reduce_scatter | solution.py:47
  234.4 224.1 %reduce-scatter.14.cloned.1.call-start = ((), (), s32[]{:S(2)}) async-start(), calls=%async_computation.11 | async-start | bytes 3342336 | tf_op jit(solution)/shard_map/reduce_scatter | solution.py:47
  243.6 136.0 %copy-start = (f32[3,512,512]{2,1,0:T(8,128)S(1)}, f32[3,512,512]{2,1,0:T(8,128)}, u32[]{:S(2)}) copy-start(f32[3,512,512]{2,1,0:T(8,128)} %param.7) | copy-start | bytes 9437188
  243.6 395.3 %all-reduce.5.cloned.1.call-start = ((), (), s32[]{:S(2)}) async-start(), calls=%async_computation.12 | async-start | bytes 12582912 | tf_op jit(solution)/shard_map/psum | solution.py:56
  301.2 159.9 %copy-start.16 = (f32[96,512]{1,0:T(8,128)S(1)}, f32[96,512]{1,0:T(8,128)}, u32[]{:S(2)}) copy-start(f32[96,512]{1,0:T(8,128)} %reduce-scatter.10.cloned.1.call-done) | copy-start | bytes 589828
  458.6 3.3 copy-start.20
  458.6 5.7 copy-start.22
  461.1 6.2 copy-start.17
  461.9 5.5 copy-start.19
  461.9 5.5 copy-start.21
  469.0 0.9 copy-start.18
  475.2 22.3 %all-to-all-start = ((f32[3,8,12,512]{3,2,0,1:T(8,128)}), f32[3,8,12,512]{3,2,0,1:T(8,128)}, u32[]{:S(2)}, u32[]{:S(2)}) async-start(f32[3,8,12,512]{3,2,0,1:T(8,128)} %copy.78), calls=%async_computation | async-start | bytes 1572864 | tf_op jit(solution)/shard_map/all_to_all | solution.py:80
  501.5 25.8 %all-to-all-start.1 = ((f32[3,16,12,512]{3,2,0,1:T(8,128)}), f32[3,16,12,512]{3,2,0,1:T(8,128)}, u32[]{:S(2)}, u32[]{:S(2)}) async-start(f32[3,16,12,512]{3,2,0,1:T(8,128)} %copy.80), calls=%async_computation.1 | async-start | bytes 3145728 | tf_op jit(solution)/shard_map/all_to_all | solution.py:86
  529.4 21.4 %all-to-all-start.2 = ((f32[3,8,12,512]{3,2,0,1:T(8,128)}), f32[3,8,12,512]{3,2,0,1:T(8,128)}, u32[]{:S(2)}, u32[]{:S(2)}) async-start(f32[3,8,12,512]{3,2,0,1:T(8,128)} %constant_dynamic-slice_fusion), calls=%async_computation.2 | async-start | bytes 1572864 | tf_op jit(solution)/shard_map/all_to_all | solution.py:88
  642.7 5.8 copy-start.1
  642.7 3.8 copy-start.8
  642.7 3.8 copy-start.9
  644.6 3.9 copy-start.10
  644.6 3.9 copy-start.11
  646.6 12.5 %copy-start.3 = (f32[512,512]{0,1:T(8,128)}, f32[512,512]{0,1:T(8,128)S(1)}, u32[]{:S(2)}) copy-start(f32[512,512]{0,1:T(8,128)S(1)} %fusion.18) | copy-start | bytes 3145732
  648.5 5.1 copy-start.6
  650.5 1.0 copy-start.7
  653.7 5.4 copy-start.4
  671.3 4.3 copy-start.2
  671.3 4.3 copy-start.12
  671.3 4.3 copy-start.15
  675.7 1.2 copy-start.13
  675.7 1.5 copy-start.14
  677.2 1.9 copy-start.5
Sparse Core Ops, SparseCore 0:
  10.7 46.3 all-gather.5
  59.2 43.3 all-gather.3
  104.7 43.3 all-gather.7
  151.0 65.1 all-reduce.6
  225.4 75.7 reduce-scatter.9
  304.4 75.1 reduce-scatter.11
  383.4 75.0 reduce-scatter.13
  469.1 169.7 all-reduce.4
where the time goes:
time: 699 us; the launch traced here: 691 us
  waiting for transfers between devices  539 us (77%)
  matrix products  54.5 us (8%)
  local copies, waits for them, and re-layouts  36 us (5%)
  other arithmetic  26 us (4%)
  starting transfers between devices  21.2 us (3%)
  between operations  14.7 us (2%)
    reduce_scatter x3, waiting for transfers between devices, local(): lax.psum_scatter(matmul(ancestor_inverse, lower_cols), 'col', scatter_dim...  213 us
    all_gather x3, waiting for transfers between devices, local(): lower_rows = lax.all_gather(lower_part, 'col', axis=0, tiled=True)  132 us
    psum x1, waiting for transfers between devices, local(): summed = lax.psum(left_dot(lower_here, stacked), ('row', 'col'))  83.9 us
    psum x1, waiting for transfers between devices, broadcast(): return lax.psum(kept, axis)  66 us
    dot_general x11, matrix products, matmul(): return jnp.dot(left, right, precision=highest)  36 us
    all_to_all x1, waiting for transfers between devices, local(): lax.all_to_all(slotted, 'col', split_axis=1, concat_axis=1, tiled=True)  21 us
    dot_general x6, matrix products, left_dot(): lax.dot_general(left, right, (((0,), (0,)), ((), ())), precision=highest)  16.5 us
    all_to_all x1, waiting for transfers between devices, local(): lax.all_to_all(split_parts, 'row', split_axis=1, concat_axis=1, tiled=True)  15.6 us
  transfers between devices with their start and end apart: 11, of which 11 were waited for; matrix products, arithmetic and copies ran while one was open for 7% of the time, Pallas kernels for 0%

commit v1 on v0

--- a/solution.py
+++ b/solution.py
@@ -53,7 +53,9 @@
             )
         column = -product_sum
         stacked = jnp.concatenate(row_layout + [column], axis=1)
-        summed = lax.psum(left_dot(lower_here, stacked), ("row", "col"))
+        summed = left_dot(lower_here, stacked)
+        for m in ("col", "row"):
+            summed = lax.psum(summed, m)
         crosses = [
             summed[:, earlier * sn_width : (earlier + 1) * sn_width] for earlier in range(current)
         ]

time: 699 us -> 757 us (1.083)
  waiting for transfers between devices: 539 us -> 600 us
    psum x1 -> x2, waiting for transfers between devices: 83.9 us -> 138 us  [local(): summed = lax.psum(summed, m)]
  transfers between devices with their start and end apart: 11 -> 12, of which waited for: 11 -> 12; matrix products, arithmetic and copies ran while one was open for 7% -> 6% of each run, Pallas kernels for 0% -> 0%
where the time goes in v1:
time: 757 us; the launch traced here: 748 us
  waiting for transfers between devices  600 us (79%)
  matrix products  54.6 us (7%)
  local copies, waits for them, and re-layouts  35.7 us (5%)
  other arithmetic  25.9 us (3%)
  starting transfers between devices  18.2 us (2%)
  between operations  14.5 us (2%)
    reduce_scatter x3, waiting for transfers between devices, local(): lax.psum_scatter(matmul(ancestor_inverse, lower_cols), 'col', scatter_dim...  213 us
    psum x2, waiting for transfers between devices, local(): summed = lax.psum(summed, m)  138 us
    all_gather x3, waiting for transfers between devices, local(): lower_rows = lax.all_gather(lower_part, 'col', axis=0, tiled=True)  132 us
    psum x1, waiting for transfers between devices, broadcast(): return lax.psum(kept, axis)  66 us
    dot_general x11, matrix products, matmul(): return jnp.dot(left, right, precision=highest)  36 us
    all_to_all x1, waiting for transfers between devices, local(): lax.all_to_all(slotted, 'col', split_axis=1, concat_axis=1, tiled=True)  22.1 us
    all_to_all x1, waiting for transfers between devices, local(): lax.all_to_all(split_parts, 'row', split_axis=1, concat_axis=1, tiled=True)  16.7 us
    dot_general x6, matrix products, left_dot(): lax.dot_general(left, right, (((0,), (0,)), ((), ())), precision=highest)  16.5 us
  transfers between devices with their start and end apart: 12, of which 12 were waited for; matrix products, arithmetic and copies ran while one was open for 6% of the time, Pallas kernels for 0%

profile of v1, /device:TPU:1, one launch (start us, length us, event | category | flops | bytes accessed | tf_op | source)
XLA Modules:
  0.0 748.4 jit_solution(15477927722143181249)
XLA Ops:
  7.2 0.8 slice_bitcast_fusion.2
  8.1 1.8 bitcast_select_fusion.1
  11.5 45.6 %all-gather.6.cloned.1.call-done = bf16[1536,512]{1,0:T(8,128)(2,1)} async-done(((bf16[96,512]{1,0:T(8,128)(2,1)}), bf16[1536,512]{1,0:T(8,128)(2,1)}) %all-gather.6.cloned.1.call-update) | async-done | bytes 1572880 | tf_op jit(solution)/shard_map/all_gather | solution.py:43
  57.1 2.2 dynamic-slice_select_fusion.1
  59.2 43.3 %all-gather.4.cloned.1.call-done = bf16[1536,512]{1,0:T(8,128)(2,1)} async-done(((bf16[96,512]{1,0:T(8,128)(2,1)}), bf16[1536,512]{1,0:T(8,128)(2,1)}) %all-gather.4.cloned.1.call-update) | async-done | bytes 1572880 | tf_op jit(solution)/shard_map/all_gather | solution.py:43
  102.5 2.1 dynamic-slice_select_fusion.2
  104.7 43.4 %all-gather.8.cloned.1.call-done = bf16[1536,512]{1,0:T(8,128)(2,1)} async-done(((bf16[96,512]{1,0:T(8,128)(2,1)}), bf16[1536,512]{1,0:T(8,128)(2,1)}) %all-gather.8.cloned.1.call-update) | async-done | bytes 1572880 | tf_op jit(solution)/shard_map/all_gather | solution.py:43
  148.0 2.1 dynamic-slice_select_fusion
  150.3 66.0 %all-reduce.11.cloned.1.call-done = (bf16[768,512]{1,0:T(8,128)(2,1)}, bf16[768,512]{1,0:T(8,128)(2,1)}, bf16[768,512]{1,0:T(8,128)(2,1)}) async-done(((bf16[768,512]{1,0:T(8,128)(2,1)}, bf16[768,512]{1,0:T(8,128)(2,1)}, bf16[768,512]{1,0:T(8,128)(2,1)}), (bf16[768,512]{1,0:T(8,128)(2,1)}, bf16[768,512]{1,0:T(8,128)(2,1)}, bf16[768,512]{1,0:T(8,128)(2,1)})) %all-reduce.11.cloned.1.call-update) | async-done | bytes 2359312 | tf_op jit(solution)/shard_map/psum | solution.py:11
  216.2 6.7 convolution_bitcast_fusion.2
  222.9 2.4 copy.104
  225.3 6.7 convolution_bitcast_fusion.1
  232.0 2.4 copy.106
  234.5 6.7 convolution_bitcast_fusion
  241.2 2.4 copy.108
  244.1 57.1 %reduce-scatter.10.cloned.1.call-done = f32[96,512]{1,0:T(8,128)} async-done(((f32[1536,512]{1,0:T(8,128)}), f32[96,512]{1,0:T(8,128)}) %reduce-scatter.10.cloned.1.call-update) | async-done | bytes 196624 | tf_op jit(solution)/shard_map/reduce_scatter | solution.py:47
  301.2 78.3 %reduce-scatter.12.cloned.1.call-done = f32[96,512]{1,0:T(8,128)} async-done(((f32[1536,512]{1,0:T(8,128)}), f32[96,512]{1,0:T(8,128)}) %reduce-scatter.12.cloned.1.call-update) | async-done | bytes 196624 | tf_op jit(solution)/shard_map/reduce_scatter | solution.py:47
  379.5 1.8 fusion.5
  381.3 77.2 %reduce-scatter.14.cloned.1.call-done = f32[96,512]{1,0:T(8,128)} async-done(((f32[1536,512]{1,0:T(8,128)}), f32[96,512]{1,0:T(8,128)}) %reduce-scatter.14.cloned.1.call-update) | async-done | bytes 196624 | tf_op jit(solution)/shard_map/reduce_scatter | solution.py:47
  458.6 1.8 convolution_add_fusion.1
  460.4 0.7 fusion.4
  461.1 0.7 fusion.63
  461.8 2.4 fusion.45
  464.3 3.1 fusion.38
  467.4 1.6 fusion.54
  469.0 123.7 %all-reduce.7.cloned.1.call-done = (f32[512,1536]{1,0:T(8,128)}, f32[512,512]{1,0:T(8,128)}, f32[512,1024]{0,1:T(8,128)}) async-done(((f32[512,1536]{1,0:T(8,128)}, f32[512,512]{1,0:T(8,128)}, f32[512,1024]{0,1:T(8,128)}), (f32[512,1536]{1,0:T(8,128)}, f32[512,512]{1,0:T(8,128)}, f32[512,1024]{0,1:T(8,128)})) %all-reduce.7.cloned.1.call-update) | async-done | bytes 6291472 | tf_op jit(solution)/shard_map/psum | solution.py:58
  592.8 0.9 copy-done.18
  593.7 0.7 stack.74
  594.4 0.7 stack.73
  595.2 1.6 stack.72
  596.8 1.2 pad_maximum_fusion.1
  598.0 0.9 copy.78
  598.9 5.0 all-to-all-start
  603.9 16.7 %all-to-all-done = f32[3,8,12,512]{3,2,0,1:T(8,128)} async-done(((f32[3,8,12,512]{3,2,0,1:T(8,128)}), f32[3,8,12,512]{3,2,0,1:T(8,128)}, u32[]{:S(2)}, u32[]{:S(2)}) %all-to-all-start) | async-done | bytes 589856 | tf_op jit(solution)/shard_map/all_to_all | solution.py:82
  620.6 2.1 convolution_bitcast_fusion.3
  622.7 1.8 copy.80
  624.6 5.0 all-to-all-start.1
  629.6 22.1 %all-to-all-done.1 = f32[3,16,12,512]{3,2,0,1:T(8,128)} async-done(((f32[3,16,12,512]{3,2,0,1:T(8,128)}), f32[3,16,12,512]{3,2,0,1:T(8,128)}, u32[]{:S(2)}, u32[]{:S(2)}) %all-to-all-start.1) | async-done | bytes 1179680 | tf_op jit(solution)/shard_map/all_to_all | solution.py:88
  651.7 2.1 constant_dynamic-slice_fusion
  653.8 7.5 all-to-all-start.2
  661.3 2.3 slice.71
  663.6 2.6 copy.110
  666.1 1.8 pad_maximum_fusion.2
  667.9 10.0 %all-to-all-done.2 = f32[3,8,12,512]{3,2,0,1:T(8,128)} async-done(((f32[3,8,12,512]{3,2,0,1:T(8,128)}), f32[3,8,12,512]{3,2,0,1:T(8,128)}, u32[]{:S(2)}, u32[]{:S(2)}) %all-to-all-start.2) | async-done | bytes 589856 | tf_op jit(solution)/shard_map/all_to_all | solution.py:90
  677.9 2.1 copy.81
  680.0 2.0 reshape.46
  682.0 14.6 %all-reduce.9.cloned.1.call-done = (f32[512,1536]{1,0:T(8,128)}, f32[512,512]{1,0:T(8,128)}, f32[512,1024]{0,1:T(8,128)}) async-done(((f32[512,1536]{1,0:T(8,128)}, f32[512,512]{1,0:T(8,128)}, f32[512,1024]{0,1:T(8,128)}), (f32[512,1536]{1,0:T(8,128)}, f32[512,512]{1,0:T(8,128)}, f32[512,1024]{0,1:T(8,128)})) %all-reduce.9.cloned.1.call-update) | async-done | bytes 6291472 | tf_op jit(solution)/shard_map/psum | solution.py:58
  696.6 3.8 bitcast_subtract_fusion.7
  700.4 1.9 fusion.14
  702.3 1.9 fusion.18
  704.3 1.9 fusion.20
  706.2 2.0 fusion.3
  708.2 1.0 copy-done.7
  709.2 2.1 fusion.12
  711.4 3.1 fusion.2
  714.5 2.3 fusion.7
  716.8 2.3 fusion.60
  719.1 2.6 copy.85
  721.7 3.8 maximum_bitcast_fusion.1
  725.5 3.5 copy.95
  729.0 4.3 fusion.1
  733.7 0.9 copy-done.13
  735.2 1.6 copy-done.5
  736.8 4.9 pad_maximum_fusion
  (65 shorter events, 3.4 us)
Async XLA Ops:
  7.2 49.9 %all-gather.6.cloned.1.call-start = ((), (), s32[]{:S(2)}) async-start(), calls=%async_computation.7 | async-start | bytes 1671168 | tf_op jit(solution)/shard_map/all_gather | solution.py:43
  9.9 92.6 %all-gather.4.cloned.1.call-start = ((), (), s32[]{:S(2)}) async-start(), calls=%async_computation.6 | async-start | bytes 1671168 | tf_op jit(solution)/shard_map/all_gather | solution.py:43
  10.7 137.4 %all-gather.8.cloned.1.call-start = ((), (), s32[]{:S(2)}) async-start(), calls=%async_computation.8 | async-start | bytes 1671168 | tf_op jit(solution)/shard_map/all_gather | solution.py:43
  11.4 204.8 %all-reduce.11.cloned.1.call-start = ((), (), s32[]{:S(2)}) async-start(), calls=%async_computation.14 | async-start | bytes 4718592 | tf_op jit(solution)/shard_map/psum | solution.py:11
  150.2 151.0 %reduce-scatter.10.cloned.1.call-start = ((), (), s32[]{:S(2)}) async-start(), calls=%async_computation.9 | async-start | bytes 3342336 | tf_op jit(solution)/shard_map/reduce_scatter | solution.py:47
  225.3 154.3 %reduce-scatter.12.cloned.1.call-start = ((), (), s32[]{:S(2)}) async-start(), calls=%async_computation.10 | async-start | bytes 3342336 | tf_op jit(solution)/shard_map/reduce_scatter | solution.py:47
  234.5 224.1 %reduce-scatter.14.cloned.1.call-start = ((), (), s32[]{:S(2)}) async-start(), calls=%async_computation.11 | async-start | bytes 3342336 | tf_op jit(solution)/shard_map/reduce_scatter | solution.py:47
  243.6 136.0 %copy-start = (f32[3,512,512]{2,1,0:T(8,128)S(1)}, f32[3,512,512]{2,1,0:T(8,128)}, u32[]{:S(2)}) copy-start(f32[3,512,512]{2,1,0:T(8,128)} %param.7) | copy-start | bytes 9437188
  243.6 349.2 %all-reduce.7.cloned.1.call-start = ((), (), s32[]{:S(2)}) async-start(), calls=%async_computation.12 | async-start | bytes 12582912 | tf_op jit(solution)/shard_map/psum | solution.py:58
  301.2 159.9 %copy-start.16 = (f32[96,512]{1,0:T(8,128)S(1)}, f32[96,512]{1,0:T(8,128)}, u32[]{:S(2)}) copy-start(f32[96,512]{1,0:T(8,128)} %reduce-scatter.10.cloned.1.call-done) | copy-start | bytes 589828
  458.6 3.3 copy-start.20
  458.6 5.7 copy-start.22
  461.1 6.2 copy-start.17
  461.8 5.5 copy-start.19
  461.8 5.5 copy-start.21
  469.0 227.6 %all-reduce.9.cloned.1.call-start = ((), (), s32[]{:S(2)}) async-start(), calls=%async_computation.13 | async-start | bytes 12582912 | tf_op jit(solution)/shard_map/psum | solution.py:58
  592.8 0.9 copy-start.18
  598.9 21.7 %all-to-all-start = ((f32[3,8,12,512]{3,2,0,1:T(8,128)}), f32[3,8,12,512]{3,2,0,1:T(8,128)}, u32[]{:S(2)}, u32[]{:S(2)}) async-start(f32[3,8,12,512]{3,2,0,1:T(8,128)} %copy.78), calls=%async_computation | async-start | bytes 1572864 | tf_op jit(solution)/shard_map/all_to_all | solution.py:82
  624.6 27.1 %all-to-all-start.1 = ((f32[3,16,12,512]{3,2,0,1:T(8,128)}), f32[3,16,12,512]{3,2,0,1:T(8,128)}, u32[]{:S(2)}, u32[]{:S(2)}) async-start(f32[3,16,12,512]{3,2,0,1:T(8,128)} %copy.80), calls=%async_computation.1 | async-start | bytes 3145728 | tf_op jit(solution)/shard_map/all_to_all | solution.py:88
  653.8 24.2 %all-to-all-start.2 = ((f32[3,8,12,512]{3,2,0,1:T(8,128)}), f32[3,8,12,512]{3,2,0,1:T(8,128)}, u32[]{:S(2)}, u32[]{:S(2)}) async-start(f32[3,8,12,512]{3,2,0,1:T(8,128)} %constant_dynamic-slice_fusion), calls=%async_computation.2 | async-start | bytes 1572864 | tf_op jit(solution)/shard_map/all_to_all | solution.py:90
  700.4 5.8 copy-start.1
  700.4 3.8 copy-start.8
  700.4 3.8 copy-start.9
  702.3 3.9 copy-start.10
  702.3 3.9 copy-start.11
  704.3 12.5 %copy-start.3 = (f32[512,512]{0,1:T(8,128)}, f32[512,512]{0,1:T(8,128)S(1)}, u32[]{:S(2)}) copy-start(f32[512,512]{0,1:T(8,128)S(1)} %fusion.18) | copy-start | bytes 3145732
  706.2 5.1 copy-start.6
  708.2 1.0 copy-start.7
  711.4 5.5 copy-start.4
  729.0 4.3 copy-start.2
  729.0 4.3 copy-start.12
  729.0 4.3 copy-start.15
  733.4 1.2 copy-start.13
  733.4 1.5 copy-start.14
  734.9 1.9 copy-start.5
Sparse Core Ops, SparseCore 0:
  10.7 46.3 all-gather.5
  59.2 43.3 all-gather.3
  104.7 43.3 all-gather.7
  151.0 65.1 all-reduce.10
  225.4 75.7 reduce-scatter.9
  304.4 75.0 reduce-scatter.11
  383.4 75.0 reduce-scatter.13
  469.1 123.6 all-reduce.6
  595.5 101.1 all-reduce.8
